TPU v7x, 256 devices: a whole 4x4x8 slice. The times are simulated.
256 devices in a mesh: slot: 8 (over y, core), asset: 32 (over x, z).
Axes of the slice: x: 4, y: 4, z: 8, core: 2. Of those that a mesh axis runs over, the one named last changes fastest.
Arguments:
- slot_emb: bfloat16 [16384, 768], P(('slot', 'asset')), may hold values from -4 to 4
- asset_panel: bfloat16 [768, 32768], P('slot', 'asset'), may hold values from -4 to 4
- mult: int32 [16384], P('slot'), may hold values from 1 to 4
- caps: int32 [32768], P('asset'), may hold values from 1 to 8, as said below
Outputs:
- plan: float32 [16384, 32768], P('slot', 'asset')
Inputs may be any that keep to these rules, and one draw needn't show every extreme that they name: caps are whole numbers; the last asset's cap is the largest.
All inputs are finite; a program needn't handle non-finite values.
Results may differ from a plain program's by a relative error of at most 0.0003.
Values may be sent and summed in bfloat16 or wider, within the bound.
No kernel may reach another device: no remote copies, remote signals or barrier semaphores. Data moves between devices by JAX's collectives and lax.ppermute only.
A program may use at most 64 MiB of HBM per device.

v0:
```python
import jax
import jax.numpy as jnp
from jax import lax
from jax.sharding import PartitionSpec as P

EMB = 768
ITERS = 3


def row_side(logits, asset_pot):
    shifted = logits + asset_pot[None, :]
    peak = lax.pmax(jnp.max(shifted, axis=1), "asset")
    total = lax.psum(jnp.sum(jnp.exp(shifted - peak[:, None]), axis=1), "asset")
    return peak + jnp.log(total)


def col_side(logits, slot_pot):
    shifted = logits + slot_pot[:, None]
    peak = lax.pmax(jnp.max(shifted, axis=0), "slot")
    total = lax.psum(jnp.sum(jnp.exp(shifted - peak[None, :]), axis=0), "slot")
    return peak + jnp.log(total)


def per_device(slot_emb, asset_panel, mult, caps):
    slot_block = lax.all_gather(slot_emb, "asset", axis=0, tiled=True)
    logits = jnp.dot(
        slot_block,
        lax.all_gather(asset_panel, "slot", axis=0, tiled=True),
        preferred_element_type=jnp.float32,
    ) * EMB ** (-0.5)
    caps_float = caps.astype(jnp.float32)
    cap_total = lax.psum(jnp.sum(caps_float), "asset")
    log_b = jnp.log(caps_float) - jnp.log(cap_total)
    log_a = jnp.log(mult.astype(jnp.float32))
    asset_pot = jnp.zeros((logits.shape[1],), jnp.float32)
    slot_pot = jnp.zeros((logits.shape[0],), jnp.float32)
    for iteration in range(ITERS):
        slot_pot = log_a - row_side(logits, asset_pot)
        asset_pot = log_b - col_side(logits, slot_pot)
    factor = float(
        logits.shape[0] * lax.axis_size("slot") * logits.shape[1] * lax.axis_size("asset")
    )
    return jnp.exp(logits + slot_pot[:, None] + asset_pot[None, :]) * factor


def solution(mesh):
    return jax.shard_map(
        per_device,
        mesh=mesh,
        in_specs=(P(("slot", "asset"), None), P("slot", "asset"), P("slot"), P("asset")),
        out_specs=P("slot", "asset"),
        check_vma=False,
    )
```

profile of v0, /device:TPU:1, one launch (start us, length us, event | category | flops | bytes accessed | tf_op | source)
XLA Modules:
  0.0 697.3 jit_solution(16595806168147780768)
XLA Ops:
  6.5 0.7 all-gather.5.cloned.1.call-update
  7.3 0.0 all-gather.3.cloned.1.call-start
  7.3 0.7 all-gather.3.cloned.1.call-update
  8.0 1.3 convert_reduce_fusion
  9.3 31.0 %all-gather.5.cloned.1.call-done = bf16[768,1024]{1,0:T(8,128)(2,1)} async-done(((bf16[96,1024]{1,0:T(8,128)(2,1)}), bf16[768,1024]{1,0:T(8,128)(2,1)}) %all-gather.5.cloned.1.call-update) | async-done | bytes 1572880 | tf_op jit(solution)/shard_map/all_gather | solution.py:28
  40.3 77.9 %all-gather.3.cloned.1.call-done = bf16[2048,768]{1,0:T(8,128)(2,1)} async-done(((bf16[64,768]{1,0:T(8,128)(2,1)}), bf16[2048,768]{1,0:T(8,128)(2,1)}) %all-gather.3.cloned.1.call-update) | async-done | bytes 3145744 | tf_op jit(solution)/shard_map/all_gather | solution.py:25
  118.2 9.2 %fusion = (f32[2048]{0:T(1024)S(1)}, f32[2048,1024]{1,0:T(8,128)}) fusion(bf16[2048,768]{1,0:T(8,128)(2,1)} %all-gather.3.cloned.1.call-done, bf16[768,1024]{1,0:T(8,128)(2,1)} %all-gather.5.cloned.1.call-done), kind=kOutput, calls=%fused_computation.22 | convolution fusion | flops 3225417728 | bytes 13115392 | tf_op jit(solution)/shard_map/dot_general | solution.py:26
  127.4 58.9 %pmax.42 = f32[2048]{0:T(1024)S(1)} all-reduce(f32[2048]{0:T(1024)S(1)} %get-tuple-element.7), channel_id=1, replica_groups=mesh['slot'=8,'asset'=32] {'asset'}, use_global_device_ids=true, to_apply=%region_3.0 | all-reduce | flops 2048 | bytes 16384 | tf_op jit(solution)/shard_map/pmax | solution.py:12
  186.3 4.4 exponential_reduce_fusion.5
  190.7 58.3 %all-reduce = (f32[2048]{0:T(1024)S(1)}, f32[]{:T(128)}) all-reduce(f32[2048]{0:T(1024)S(1)} %exponential_reduce_fusion.5, f32[]{:T(128)} %convert_reduce_fusion), channel_id=1, replica_groups=mesh['slot'=8,'asset'=32] {'asset'}, use_global_device_ids=true, to_apply=%region_5.0 | all-reduce | flops 2049 | bytes 16392 | tf_op jit(solution)/shard_map/psum | solution.py:13
  249.6 0.0 copy-start.1
  249.6 4.0 add_reduce_fusion.3
  253.6 44.0 %pmax.43 = f32[1024]{0:T(1024)S(1)} all-reduce(f32[1024]{0:T(1024)S(1)} %add_reduce_fusion.3), channel_id=1, replica_groups=mesh['slot'=8,'asset'=32] {'slot'}, use_global_device_ids=true, to_apply=%region_7.0 | all-reduce | flops 1024 | bytes 8192 | tf_op jit(solution)/shard_map/pmax | solution.py:19
  297.6 4.2 exponential_reduce_fusion.4
  301.9 12.4 %psum.51 = f32[1024]{0:T(1024)S(1)} all-reduce(f32[1024]{0:T(1024)S(1)} %exponential_reduce_fusion.4), channel_id=1, replica_groups=mesh['slot'=8,'asset'=32] {'slot'}, use_global_device_ids=true, to_apply=%region_9.0 | all-reduce | flops 1024 | bytes 8192 | tf_op jit(solution)/shard_map/psum | solution.py:20
  314.3 4.0 add_reduce_fusion.2
  318.3 59.1 %pmax.44 = f32[2048]{0:T(1024)S(1)} all-reduce(f32[2048]{0:T(1024)S(1)} %add_reduce_fusion.2), channel_id=1, replica_groups=mesh['slot'=8,'asset'=32] {'asset'}, use_global_device_ids=true, to_apply=%region_11.0 | all-reduce | flops 2048 | bytes 16384 | tf_op jit(solution)/shard_map/pmax | solution.py:12
  377.5 4.4 exponential_reduce_fusion.3
  381.8 57.1 %psum.52 = f32[2048]{0:T(1024)S(1)} all-reduce(f32[2048]{0:T(1024)S(1)} %exponential_reduce_fusion.3), channel_id=1, replica_groups=mesh['slot'=8,'asset'=32] {'asset'}, use_global_device_ids=true, to_apply=%region_13.0 | all-reduce | flops 2048 | bytes 16384 | tf_op jit(solution)/shard_map/psum | solution.py:13
  438.9 4.0 add_reduce_fusion.1
  442.9 39.6 %pmax.45 = f32[1024]{0:T(1024)S(1)} all-reduce(f32[1024]{0:T(1024)S(1)} %add_reduce_fusion.1), channel_id=1, replica_groups=mesh['slot'=8,'asset'=32] {'slot'}, use_global_device_ids=true, to_apply=%region_15.0 | all-reduce | flops 1024 | bytes 8192 | tf_op jit(solution)/shard_map/pmax | solution.py:19
  482.5 4.2 exponential_reduce_fusion.2
  486.8 12.4 %psum.53 = f32[1024]{0:T(1024)S(1)} all-reduce(f32[1024]{0:T(1024)S(1)} %exponential_reduce_fusion.2), channel_id=1, replica_groups=mesh['slot'=8,'asset'=32] {'slot'}, use_global_device_ids=true, to_apply=%region_17.0 | all-reduce | flops 1024 | bytes 8192 | tf_op jit(solution)/shard_map/psum | solution.py:20
  499.2 4.0 add_reduce_fusion
  503.2 59.2 %pmax.46 = f32[2048]{0:T(1024)S(1)} all-reduce(f32[2048]{0:T(1024)S(1)} %add_reduce_fusion), channel_id=1, replica_groups=mesh['slot'=8,'asset'=32] {'asset'}, use_global_device_ids=true, to_apply=%region_19.0 | all-reduce | flops 2048 | bytes 16384 | tf_op jit(solution)/shard_map/pmax | solution.py:12
  562.4 4.4 exponential_reduce_fusion.1
  566.7 57.0 %psum.54 = f32[2048]{0:T(1024)S(1)} all-reduce(f32[2048]{0:T(1024)S(1)} %exponential_reduce_fusion.1), channel_id=1, replica_groups=mesh['slot'=8,'asset'=32] {'asset'}, use_global_device_ids=true, to_apply=%region_21.0 | all-reduce | flops 2048 | bytes 16384 | tf_op jit(solution)/shard_map/psum | solution.py:13
  623.8 4.0 add_reduce_fusion.4
  627.8 39.6 %pmax.47 = f32[1024]{0:T(1024)S(1)} all-reduce(f32[1024]{0:T(1024)S(1)} %add_reduce_fusion.4), channel_id=1, replica_groups=mesh['slot'=8,'asset'=32] {'slot'}, use_global_device_ids=true, to_apply=%region_23.0 | all-reduce | flops 1024 | bytes 8192 | tf_op jit(solution)/shard_map/pmax | solution.py:19
  667.4 4.2 exponential_reduce_fusion
  671.7 12.4 %psum.55 = f32[1024]{0:T(1024)S(1)} all-reduce(f32[1024]{0:T(1024)S(1)} %exponential_reduce_fusion), channel_id=1, replica_groups=mesh['slot'=8,'asset'=32] {'slot'}, use_global_device_ids=true, to_apply=%region_25.0 | all-reduce | flops 1024 | bytes 8192 | tf_op jit(solution)/shard_map/psum | solution.py:20
  684.1 6.3 exponential_multiply_fusion
  (10 shorter events, 0.1 us)
Async XLA Ops:
  6.5 33.7 %all-gather.5.cloned.1.call-start = ((), (), s32[]{:S(2)}) async-start(), calls=%async_computation.1 | async-start | bytes 1769472 | tf_op jit(solution)/shard_map/all_gather | solution.py:28
  7.3 110.9 %all-gather.3.cloned.1.call-start = ((), (), s32[]{:S(2)}) async-start(), calls=%async_computation | async-start | bytes 3244032 | tf_op jit(solution)/shard_map/all_gather | solution.py:25
  127.4 122.2 %copy-start = (s32[2048]{0:T(1024)S(1)}, s32[2048]{0:T(1024)}, u32[]{:S(2)}) copy-start(s32[2048]{0:T(1024)} %param.6) | copy-start | bytes 24580
  249.6 64.7 %copy-start.1 = (s32[1024]{0:T(1024)S(1)}, s32[1024]{0:T(1024)}, u32[]{:S(2)}) copy-start(s32[1024]{0:T(1024)} %param.7) | copy-start | bytes 12292
Sparse Core Ops, SparseCore 0:
  9.2 31.0 all-gather.4
  42.8 75.2 all-gather.2
where the time goes:
time: 698 us; the launch traced here: 697 us
  blocking collectives  510 us (73%)
  waiting for transfers between devices  110 us (16%)
  other arithmetic  53.5 us (8%)
  between operations  14.2 us (2%)
  matrix products  9.19 us (1%)
    pmax x3, blocking collectives, row_side(): peak = lax.pmax(jnp.max(shifted, axis=1), 'asset')  177 us
    psum x3, blocking collectives, row_side(): total = lax.psum(jnp.sum(jnp.exp(shifted - peak[:, None]), axis=1), 'asset')  172 us
    pmax x3, blocking collectives, col_side(): peak = lax.pmax(jnp.max(shifted, axis=0), 'slot')  123 us
    all_gather x1, waiting for transfers between devices, per_device(): slot_block = lax.all_gather(slot_emb, 'asset', axis=0, tiled=True)  77.9 us
    psum x3, blocking collectives, col_side(): total = lax.psum(jnp.sum(jnp.exp(shifted - peak[None, :]), axis=0), 'slot')  37.3 us
    all_gather x1, waiting for transfers between devices, per_device(): lax.all_gather(asset_panel, 'slot', axis=0, tiled=True)  31 us
  transfers between devices with their start and end apart: 2, of which 2 were waited for; matrix products, arithmetic and copies ran while one was open for 0% of the time, Pallas kernels for 0%

commit v1 on v0

--- a/solution.py
+++ b/solution.py
@@ -7,10 +7,16 @@
 ITERS = 3
 
 
+def gather_and_add(x, axis):
+    pieces = lax.all_gather(x, axis, axis=0, tiled=False)
+    summed = pieces.sum(axis=0)
+    return summed
+
+
 def row_side(logits, asset_pot):
     shifted = logits + asset_pot[None, :]
     peak = lax.pmax(jnp.max(shifted, axis=1), "asset")
-    total = lax.psum(jnp.sum(jnp.exp(shifted - peak[:, None]), axis=1), "asset")
+    total = gather_and_add(jnp.sum(jnp.exp(shifted - peak[:, None]), axis=1), "asset")
     return peak + jnp.log(total)
 
 

time: 698 us -> 624 us (0.89)
  waiting for transfers between devices: 110 us -> 44.6 us
  blocking collectives: 510 us -> 501 us
    psum x3 -> x1, blocking collectives: 172 us -> 65 us  [per_device(): cap_total = lax.psum(jnp.sum(caps_float), 'asset')]
    all_gather x0 -> x3, blocking collectives: none -> 103 us  [gather_and_add(): pieces = lax.all_gather(x, axis, axis=0, tiled=False)]
    all_gather x1, waiting for transfers between devices: 77.9 us -> 43.2 us  [per_device(): slot_block = lax.all_gather(slot_emb, 'asset', axis=0, tiled=True)]
    all_gather x1, waiting for transfers between devices: 31 us -> 0.02 us  [per_device(): lax.all_gather(asset_panel, 'slot', axis=0, tiled=True)]
  transfers between devices with their start and end apart: 2 -> 2, of which waited for: 2 -> 1; matrix products, arithmetic and copies ran while one was open for 0% -> 0% of each run, Pallas kernels for 0% -> 0%
where the time goes in v1:
time: 624 us; the launch traced here: 623 us
  blocking collectives  501 us (80%)
  other arithmetic  53.6 us (9%)
  waiting for transfers between devices  44.6 us (7%)
  between operations  14.3 us (2%)
  matrix products  9.19 us (1%)
    pmax x3, blocking collectives, row_side(): peak = lax.pmax(jnp.max(shifted, axis=1), 'asset')  177 us
    pmax x3, blocking collectives, col_side(): peak = lax.pmax(jnp.max(shifted, axis=0), 'slot')  119 us
    all_gather x3, blocking collectives, gather_and_add(): pieces = lax.all_gather(x, axis, axis=0, tiled=False)  103 us
    psum x1, blocking collectives, per_device(): cap_total = lax.psum(jnp.sum(caps_float), 'asset')  65 us
    all_gather x1, waiting for transfers between devices, per_device(): slot_block = lax.all_gather(slot_emb, 'asset', axis=0, tiled=True)  43.2 us
    psum x3, blocking collectives, col_side(): total = lax.psum(jnp.sum(jnp.exp(shifted - peak[None, :]), axis=0), 'slot')  37.3 us
    reduce_sum x3, other arithmetic, row_side(): jnp.sum(jnp.exp(shifted - peak[:, None]), axis=1)  13.1 us
    reduce_sum x3, other arithmetic, col_side(): total = lax.psum(jnp.sum(jnp.exp(shifted - peak[None, :]), axis=0), 'slot')  12.7 us
  transfers between devices with their start and end apart: 2, of which 1 were waited for; matrix products, arithmetic and copies ran while one was open for 0% of the time, Pallas kernels for 0%

profile of v1, /device:TPU:1, one launch (start us, length us, event | category | flops | bytes accessed | tf_op | source)
XLA Modules:
  0.0 623.1 jit_solution(16454360630567004991)
XLA Ops:
  6.5 0.7 all-gather.8.cloned.1.call-update
  7.3 0.0 all-gather.6.cloned.1.call-start
  7.3 0.7 all-gather.6.cloned.1.call-update
  8.0 1.3 convert_reduce_fusion
  9.3 65.0 %psum.28 = f32[]{:T(128)} all-reduce(f32[]{:T(128)} %convert_reduce_fusion), channel_id=1, replica_groups=mesh['slot'=8,'asset'=32] {'asset'}, use_global_device_ids=true, to_apply=%region_1.0 | all-reduce | flops 1 | bytes 8 | tf_op jit(solution)/shard_map/psum | solution.py:38
  75.0 0.0 all-gather.8.cloned.1.call-done
  75.0 43.2 %all-gather.6.cloned.1.call-done = bf16[2048,768]{1,0:T(8,128)(2,1)} async-done(((bf16[64,768]{1,0:T(8,128)(2,1)}), bf16[2048,768]{1,0:T(8,128)(2,1)}) %all-gather.6.cloned.1.call-update) | async-done | bytes 3145744 | tf_op jit(solution)/shard_map/all_gather | solution.py:31
  118.2 9.2 %fusion = (f32[2048]{0:T(1024)S(1)}, f32[2048,1024]{1,0:T(8,128)}) fusion(bf16[2048,768]{1,0:T(8,128)(2,1)} %all-gather.6.cloned.1.call-done, bf16[768,1024]{1,0:T(8,128)(2,1)} %all-gather.8.cloned.1.call-done), kind=kOutput, calls=%fused_computation.22 | convolution fusion | flops 3225417728 | bytes 13115392 | tf_op jit(solution)/shard_map/dot_general | solution.py:32
  127.4 58.9 %pmax.42 = f32[2048]{0:T(1024)S(1)} all-reduce(f32[2048]{0:T(1024)S(1)} %get-tuple-element.5), channel_id=1, replica_groups=mesh['slot'=8,'asset'=32] {'asset'}, use_global_device_ids=true, to_apply=%region_3.0 | all-reduce | flops 2048 | bytes 16384 | tf_op jit(solution)/shard_map/pmax | solution.py:18
  186.3 4.4 exponential_reduce_fusion.5
  190.7 34.4 %all-gather = f32[65536]{0:T(1024)S(1)} all-gather(f32[2048]{0:T(1024)S(1)} %exponential_reduce_fusion.5), channel_id=2, replica_groups=mesh['slot'=8,'asset'=32] {'asset'}, dimensions={0}, use_global_device_ids=true | all-gather | bytes 270336 | tf_op jit(solution)/shard_map/all_gather | solution.py:11
  225.2 4.0 add_reduce_fusion.3
  229.2 41.9 %pmax.43 = f32[1024]{0:T(1024)S(1)} all-reduce(f32[1024]{0:T(1024)S(1)} %add_reduce_fusion.3), channel_id=1, replica_groups=mesh['slot'=8,'asset'=32] {'slot'}, use_global_device_ids=true, to_apply=%region_7.0 | all-reduce | flops 1024 | bytes 8192 | tf_op jit(solution)/shard_map/pmax | solution.py:25
  271.1 4.2 exponential_reduce_fusion.4
  275.3 12.4 %psum.29 = f32[1024]{0:T(1024)S(1)} all-reduce(f32[1024]{0:T(1024)S(1)} %exponential_reduce_fusion.4), channel_id=1, replica_groups=mesh['slot'=8,'asset'=32] {'slot'}, use_global_device_ids=true, to_apply=%region_9.0 | all-reduce | flops 1024 | bytes 8192 | tf_op jit(solution)/shard_map/psum | solution.py:26
  287.8 4.0 add_reduce_fusion.2
  291.8 59.1 %pmax.44 = f32[2048]{0:T(1024)S(1)} all-reduce(f32[2048]{0:T(1024)S(1)} %add_reduce_fusion.2), channel_id=1, replica_groups=mesh['slot'=8,'asset'=32] {'asset'}, use_global_device_ids=true, to_apply=%region_11.0 | all-reduce | flops 2048 | bytes 16384 | tf_op jit(solution)/shard_map/pmax | solution.py:18
  350.9 4.4 exponential_reduce_fusion.3
  355.3 34.2 %all-gather.1 = f32[65536]{0:T(1024)S(1)} all-gather(f32[2048]{0:T(1024)S(1)} %exponential_reduce_fusion.3), channel_id=3, replica_groups=mesh['slot'=8,'asset'=32] {'asset'}, dimensions={0}, use_global_device_ids=true | all-gather | bytes 270336 | tf_op jit(solution)/shard_map/all_gather | solution.py:11
  389.6 4.0 add_reduce_fusion.1
  393.6 38.4 %pmax.45 = f32[1024]{0:T(1024)S(1)} all-reduce(f32[1024]{0:T(1024)S(1)} %add_reduce_fusion.1), channel_id=1, replica_groups=mesh['slot'=8,'asset'=32] {'slot'}, use_global_device_ids=true, to_apply=%region_15.0 | all-reduce | flops 1024 | bytes 8192 | tf_op jit(solution)/shard_map/pmax | solution.py:25
  432.1 4.2 exponential_reduce_fusion.2
  436.3 12.4 %psum.30 = f32[1024]{0:T(1024)S(1)} all-reduce(f32[1024]{0:T(1024)S(1)} %exponential_reduce_fusion.2), channel_id=1, replica_groups=mesh['slot'=8,'asset'=32] {'slot'}, use_global_device_ids=true, to_apply=%region_17.0 | all-reduce | flops 1024 | bytes 8192 | tf_op jit(solution)/shard_map/psum | solution.py:26
  448.7 4.0 add_reduce_fusion
  452.8 59.3 %pmax.46 = f32[2048]{0:T(1024)S(1)} all-reduce(f32[2048]{0:T(1024)S(1)} %add_reduce_fusion), channel_id=1, replica_groups=mesh['slot'=8,'asset'=32] {'asset'}, use_global_device_ids=true, to_apply=%region_19.0 | all-reduce | flops 2048 | bytes 16384 | tf_op jit(solution)/shard_map/pmax | solution.py:18
  512.1 4.4 exponential_reduce_fusion.1
  516.4 34.2 %all-gather.2 = f32[65536]{0:T(1024)S(1)} all-gather(f32[2048]{0:T(1024)S(1)} %exponential_reduce_fusion.1), channel_id=4, replica_groups=mesh['slot'=8,'asset'=32] {'asset'}, dimensions={0}, use_global_device_ids=true | all-gather | bytes 270336 | tf_op jit(solution)/shard_map/all_gather | solution.py:11
  550.8 4.0 add_reduce_fusion.4
  554.8 38.4 %pmax.47 = f32[1024]{0:T(1024)S(1)} all-reduce(f32[1024]{0:T(1024)S(1)} %add_reduce_fusion.4), channel_id=1, replica_groups=mesh['slot'=8,'asset'=32] {'slot'}, use_global_device_ids=true, to_apply=%region_23.0 | all-reduce | flops 1024 | bytes 8192 | tf_op jit(solution)/shard_map/pmax | solution.py:25
  593.2 4.2 exponential_reduce_fusion
  597.5 12.4 %psum.31 = f32[1024]{0:T(1024)S(1)} all-reduce(f32[1024]{0:T(1024)S(1)} %exponential_reduce_fusion), channel_id=1, replica_groups=mesh['slot'=8,'asset'=32] {'slot'}, use_global_device_ids=true, to_apply=%region_25.0 | all-reduce | flops 1024 | bytes 8192 | tf_op jit(solution)/shard_map/psum | solution.py:26
  609.9 6.3 %exponential_multiply_fusion = f32[2048,1024]{1,0:T(8,128)} fusion(f32[2048,1024]{1,0:T(8,128)} %get-tuple-element.6, f32[1024]{0:T(1024)S(1)} %add_subtract_fusion.3, f32[2048]{0:T(1024)S(1)} %add_subtract_fusion), kind=kLoop, calls=%fused_computation | loop fusion | flops 6291456 | bytes 16789504 | tf_op jit(solution)/shard_map/mul | solution.py:49
  (17 shorter events, 0.3 us)
Async XLA Ops:
  6.5 68.5 %all-gather.8.cloned.1.call-start = ((), (), s32[]{:S(2)}) async-start(), calls=%async_computation.1 | async-start | bytes 1769472 | tf_op jit(solution)/shard_map/all_gather | solution.py:34
  7.3 110.9 %all-gather.6.cloned.1.call-start = ((), (), s32[]{:S(2)}) async-start(), calls=%async_computation | async-start | bytes 3244032 | tf_op jit(solution)/shard_map/all_gather | solution.py:31
  127.4 97.8 %copy-start = (s32[2048]{0:T(1024)S(1)}, s32[2048]{0:T(1024)}, u32[]{:S(2)}) copy-start(s32[2048]{0:T(1024)} %param.6) | copy-start | bytes 24580
  225.2 62.6 %copy-start.1 = (s32[1024]{0:T(1024)S(1)}, s32[1024]{0:T(1024)}, u32[]{:S(2)}) copy-start(s32[1024]{0:T(1024)} %param.7) | copy-start | bytes 12292
Sparse Core Ops, SparseCore 0:
  9.2 31.0 all-gather.7
  42.8 75.2 all-gather.5
